TPU v7x, 32 devices: a whole 2x2x4 slice. The times are simulated.
32 devices in a mesh: vocab: 8 (over y, x, core), hidden: 4 (over z).
Axes of the slice: x: 2, y: 2, z: 4, core: 2. Of those that a mesh axis runs over, the one named last changes fastest.
Arguments:
- token_ids: int32 [4096], P('vocab'), may hold values from 0 to 30719
- table: bfloat16 [30720, 128], P('vocab'), may hold values from -0.25 to 0.25
- projection: bfloat16 [128, 4096], P(None, 'hidden'), may hold values from -0.09375 to 0.09375
- grad_out: bfloat16 [4096, 4096], P('vocab', 'hidden'), may hold values from -6 to 6
Outputs:
- table_grad: float32 [30720, 128], P('vocab', 'hidden')
- projection_grad: float32 [128, 4096], P(None, 'hidden')
All inputs are finite; a program needn't handle non-finite values.
Results may differ from a plain program's by a relative error of at most 0.018.
Values may be sent and summed in bfloat16 or wider, within the bound.
A program may use at most 64 MiB of HBM per device.

v0:
```python
import jax
import jax.numpy as jnp
from jax import lax
from jax.sharding import PartitionSpec as P


def lookup_rows(token_ids, piece):
    count = piece.shape[0]
    inside = (token_ids >= 0) & (token_ids < count)
    picked = jnp.take(piece, jnp.clip(token_ids, 0, count - 1), axis=0)
    return jnp.where(inside[:, None], picked.astype(jnp.float32), 0.0)


def owner_rows(row_count, own_start, carry, pieces):
    grads_piece, ids_piece = pieces
    length = ids_piece.shape[0]
    row_ids = own_start + lax.iota(jnp.int32, row_count)

    def one_block(grads_block, ids_block):
        one_hot = (row_ids[:, None] == ids_block[None, :]).astype(jnp.bfloat16)
        return jnp.dot(one_hot, grads_block, preferred_element_type=jnp.float32)

    block = 2048
    grads_blocks = grads_piece.reshape(length // block, block, grads_piece.shape[1])
    ids_blocks = ids_piece.reshape(length // block, block)

    def scan_step(total, items):
        return (total + one_block(items[0], items[1]), None)

    total, unused = lax.scan(scan_step, carry, (grads_blocks, ids_blocks))
    return total


def on_device(token_ids, table, projection, grad_out):
    partial_grad = jnp.dot(grad_out, projection.T, preferred_element_type=jnp.float32)
    rounded = partial_grad.astype(jnp.bfloat16)
    token_grad = (
        lax.psum_scatter(rounded, "hidden", scatter_dimension=1, tiled=True)
        .astype(jnp.float32)
        .astype(jnp.bfloat16)
    )
    row_count = table.shape[0]
    looked = lookup_rows(token_ids, lax.all_gather(table, "vocab", axis=0, tiled=True))
    embedded = looked.astype(jnp.bfloat16)
    partial_proj = jnp.dot(embedded.T, grad_out, preferred_element_type=jnp.float32)
    projection_grad = lax.psum(partial_proj.astype(jnp.bfloat16), "vocab").astype(jnp.float32)
    own_start = lax.axis_index("vocab") * row_count
    empty = jnp.zeros((row_count, token_grad.shape[1]), jnp.float32)
    table_grad = owner_rows(
        row_count,
        own_start,
        empty,
        (
            lax.all_gather(token_grad, "vocab", axis=0, tiled=True),
            lax.all_gather(token_ids, "vocab", axis=0, tiled=True),
        ),
    )
    return (table_grad, projection_grad)


def solution(mesh):
    placed = (P("vocab"), P("vocab", None), P(None, "hidden"), P("vocab", "hidden"))
    return jax.shard_map(
        on_device,
        mesh=mesh,
        in_specs=placed,
        out_specs=(P("vocab", "hidden"), P(None, "hidden")),
        check_vma=False,
    )
```

profile of v0, /device:TPU:0, one launch (start us, length us, event | category | flops | bytes accessed | tf_op | source)
XLA Modules:
  0.0 138.5 jit_solution(14183271649989522370)
XLA Ops:
  8.0 0.0 copy-start
  8.0 0.0 reduce-scatter.2.cloned.1.call-start
  8.1 1.2 copy-done
  9.2 2.1 %convolution_convert_fusion.1 = bf16[512,128]{0,1:T(8,128)(2,1)} fusion(bf16[512,1024]{1,0:T(8,128)(2,1)S(1)} %copy-done, bf16[128,1024]{1,0:T(8,128)(2,1)} %param.8), kind=kOutput, calls=%fused_computation.13 | convolution fusion | flops 134283264 | bytes 1441792 | tf_op jit(solution)/shard_map/dot_general | solution.py:35
  11.3 0.0 reduce-scatter.2.cloned.1.call-update
  11.3 0.0 all-gather.3.cloned.1.call-start
  11.4 0.5 all-gather.3.cloned.1.call-update
  11.9 0.0 all-reduce.2.cloned.1.call-start
  12.0 10.5 %all-gather = s32[8,1,512]{2,1,0:T(1,128)S(1)} all-gather(s32[1,1,512]{2,1,0:T(1,128)} %bitcast.15), channel_id=1, replica_groups=mesh['vocab'=8,'hidden'=4] {'vocab'}, dimensions={0}, use_global_device_ids=true | all-gather | bytes 18432 | tf_op jit(solution)/shard_map/all_gather | solution.py:55
  22.6 0.7 compare_select_fusion
  23.3 0.7 compare_and_fusion.1
  24.0 9.8 %reduce-scatter.2.cloned.1.call-done = bf16[512,32]{0,1:T(8,128)(2,1)} async-done(((bf16[512,128]{0,1:T(8,128)(2,1)}), bf16[512,32]{0,1:T(8,128)(2,1)}) %reduce-scatter.2.cloned.1.call-update) | async-done | bytes 32784 | tf_op jit(solution)/shard_map/reduce_scatter | solution.py:38
  33.8 9.4 %all_gather.10 = bf16[4096,32]{0,1:T(8,128)(2,1)S(1)} all-gather(bf16[512,32]{0,1:T(8,128)(2,1)} %reduce-scatter.2.cloned.1.call-done), channel_id=1, replica_groups=mesh['vocab'=8,'hidden'=4] {'vocab'}, dimensions={0}, use_global_device_ids=true | all-gather | bytes 294912 | tf_op jit(solution)/shard_map/all_gather | solution.py:54
  43.3 0.5 copy.8
  43.8 25.3 %all-gather.3.cloned.1.call-done = bf16[30720,128]{1,0:T(8,128)(2,1)} async-done(((bf16[3840,128]{1,0:T(8,128)(2,1)}), bf16[30720,128]{1,0:T(8,128)(2,1)}) %all-gather.3.cloned.1.call-update) | async-done | bytes 7864336 | tf_op jit(solution)/shard_map/all_gather | solution.py:43
  69.1 5.3 %gather_fusion = bf16[512,128]{1,0:T(8,128)(2,1)S(1)} fusion(bf16[30720,128]{1,0:T(8,128)(2,1)} %all-gather.3.cloned.1.call-done, s32[1024]{0:T(1024)S(1)} %pad_clamp_fusion), kind=kCustom, calls=%fused_computation | custom fusion | bytes 264192 | tf_op jit(solution)/shard_map/jit(_take)/gather | solution.py:10
  74.4 1.3 convolution_convert_fusion
  75.7 0.0 all-reduce.2.cloned.1.call-update
  75.7 12.5 %while.11 = (s32[]{:T(128)}, f32[3840,32]{0,1:T(8,128)S(1)}, s32[2,2048]{1,0:T(2,128)S(1)}, bf16[2,2048,32]{2,1,0:T(8,128)(2,1)S(1)}, s32[]{:T(128)}, /*index=5*/s32[]{:T(128)}, s32[]{:T(128)}) while((s32[]{:T(128)}, f32[3840,32]{0,1:T(8,128)S(1)}, s32[2,2048]{1,0:T(2,128)S(1)}, bf16[2,2048,32]{2,1,0:T(8,128)(2,1)S(1)}, s32[]{:T(128)}, ...), condition=%wide.region_2.3_spmd.clone, body=%wide.region_1.2_spmd.clone.sunk | while | flops 511430400 | bytes 1563747 | solution.py:30
  75.8 6.2 %fusion.27 = f32[3840,32]{0,1:T(8,128)S(1)} fusion(s32[2048]{0:T(1024)S(1)} %bitcast.14, s32[3840]{0:T(1024)S(1)} %iota_add_fusion.2, bf16[2,2048,32]{2,1,0:T(8,128)(2,1)S(1)} %get-tuple-element.121, s32[]{:T(128)} %get-tuple-element.111, f32[3840,32]{0,1:T(8,128)S(1)} %get-tuple-element.112, pred[]{:T(512)S(6)} %compare.3), kind=kOutput, calls=%fused_computation.6.clone.1 | convolution fusion | flops 511426560 | bytes 1531909 | tf_op jit(solution)/shard_map/while/body/eval_jaxpr/dot_general | solution.py:21
  82.1 6.2 %fusion.27 = f32[3840,32]{0,1:T(8,128)S(1)} fusion(s32[2048]{0:T(1024)S(1)} %bitcast.14, s32[3840]{0:T(1024)S(1)} %iota_add_fusion.2, bf16[2,2048,32]{2,1,0:T(8,128)(2,1)S(1)} %get-tuple-element.121, s32[]{:T(128)} %get-tuple-element.111, f32[3840,32]{0,1:T(8,128)S(1)} %get-tuple-element.112, pred[]{:T(512)S(6)} %compare.3), kind=kOutput, calls=%fused_computation.6.clone.1 | convolution fusion | flops 511426560 | bytes 1531909 | tf_op jit(solution)/shard_map/while/body/eval_jaxpr/dot_general | solution.py:21
  88.3 0.0 copy-start.1
  88.3 41.0 %all-reduce.2.cloned.1.call-done = bf16[128,1024]{1,0:T(8,128)(2,1)} async-done(((bf16[128,1024]{1,0:T(8,128)(2,1)}), bf16[128,1024]{1,0:T(8,128)(2,1)}) %all-reduce.2.cloned.1.call-update) | async-done | bytes 262160 | tf_op jit(solution)/shard_map/psum | solution.py:46
  129.3 1.8 %convert_element_type.22 = f32[128,1024]{1,0:T(8,128)} convert(bf16[128,1024]{1,0:T(8,128)(2,1)} %all-reduce.2.cloned.1.call-done) | non-fusion elementwise | flops 131072 | bytes 786432 | tf_op jit(solution)/shard_map/convert_element_type | solution.py:46
  131.1 0.0 copy-done.1
  (8 shorter events, 0.1 us)
Async XLA Ops:
  8.0 1.2 copy-start
  8.0 25.8 %reduce-scatter.2.cloned.1.call-start = ((), (), s32[]{:S(2)}) async-start(), calls=%async_computation.1 | async-start | bytes 163840 | tf_op jit(solution)/shard_map/reduce_scatter | solution.py:38
  11.3 57.8 %all-gather.3.cloned.1.call-start = ((), (), s32[]{:S(2)}) async-start(), calls=%async_computation.2 | async-start | bytes 8847360 | tf_op jit(solution)/shard_map/all_gather | solution.py:43
  11.9 117.4 %all-reduce.2.cloned.1.call-start = ((), (), s32[]{:S(2)}) async-start(), calls=%async_computation.3 | async-start | bytes 524288 | tf_op jit(solution)/shard_map/psum | solution.py:46
  88.3 42.8 %copy-start.1 = (f32[3840,32]{0,1:T(8,128)}, f32[3840,32]{0,1:T(8,128)S(1)}, u32[]{:S(2)}) copy-start(f32[3840,32]{0,1:T(8,128)S(1)} %get-tuple-element.27) | copy-start | bytes 1474564
Sparse Core Ops, SparseCore 0:
  11.6 22.1 reduce-scatter.1
Sparse Core Ops, SparseCore 1:
  13.7 55.3 all-gather.2
  75.8 53.4 all-reduce.1
where the time goes:
time: 139 us
  waiting for transfers between devices  76.7 us (55%)
  blocking collectives  20 us (14%)
  matrix products  15.8 us (11%)
  between operations  15.5 us (11%)
  local copies, waits for them, and re-layouts  6.99 us (5%)
  other arithmetic  3.25 us (2%)
    psum x1, waiting for transfers between devices, on_device(): lax.psum(partial_proj.astype(jnp.bfloat16), 'vocab').astype(jnp.float32)  41 us
    all_gather x1, waiting for transfers between devices, on_device(): lax.all_gather(table, 'vocab', axis=0, tiled=True)  25.3 us
    dot_general x2, matrix products, one_block(): return jnp.dot(one_hot, grads_block, preferred_element_type=jnp.float32)  12.4 us
    all_gather x1, blocking collectives, on_device(): lax.all_gather(token_ids, 'vocab', axis=0, tiled=True)  10.5 us
    reduce_scatter x1, waiting for transfers between devices, on_device(): lax.psum_scatter(rounded, 'hidden', scatter_dimension=1, tiled=True)  9.83 us
    all_gather x1, blocking collectives, on_device(): lax.all_gather(token_grad, 'vocab', axis=0, tiled=True)  9.44 us
    gather x1, local copies, waits for them, and re-layouts, lookup_rows(): picked = jnp.take(piece, jnp.clip(token_ids, 0, count - 1), axis=0)  5.3 us
  transfers between devices with their start and end apart: 3, of which 3 were waited for; matrix products, arithmetic and copies ran while one was open for 10% of the time, Pallas kernels for 0%

commit v1 on v0

--- a/solution.py
+++ b/solution.py
@@ -2,6 +2,11 @@
 import jax.numpy as jnp
 from jax import lax
 from jax.sharding import PartitionSpec as P
+
+
+def gather_and_add(value, name):
+    parts = lax.all_gather(value, name)
+    return jnp.sum(parts, axis=0)
 
 
 def lookup_rows(token_ids, piece):
@@ -43,7 +48,7 @@
     looked = lookup_rows(token_ids, lax.all_gather(table, "vocab", axis=0, tiled=True))
     embedded = looked.astype(jnp.bfloat16)
     partial_proj = jnp.dot(embedded.T, grad_out, preferred_element_type=jnp.float32)
-    projection_grad = lax.psum(partial_proj.astype(jnp.bfloat16), "vocab").astype(jnp.float32)
+    projection_grad = gather_and_add(partial_proj.astype(jnp.bfloat16), "vocab").astype(jnp.float32)
     own_start = lax.axis_index("vocab") * row_count
     empty = jnp.zeros((row_count, token_grad.shape[1]), jnp.float32)
     table_grad = owner_rows(

time: 139 us -> 114 us (0.82)
  waiting for transfers between devices: 76.7 us -> 53.5 us
  blocking collectives: 20 us -> 17.6 us
    psum x1 -> x0, waiting for transfers between devices: 41 us -> none  [on_device(): lax.psum(partial_proj.astype(jnp.bfloat16), 'vocab').astype(jnp.float32)]
    all_gather x1, waiting for transfers between devices: 25.3 us -> 52.7 us  [on_device(): lax.all_gather(table, 'vocab', axis=0, tiled=True)]
    reduce_scatter x1, waiting for transfers between devices: 9.83 us -> 0.03 us  [on_device(): lax.psum_scatter(rounded, 'hidden', scatter_dimension=1, tiled=True)]
    reduce_sum x0 -> x1, other arithmetic: none -> 2.13 us  [gather_and_add(): return jnp.sum(parts, axis=0)]
    all_gather x1, blocking collectives: 10.5 us -> 8.88 us  [on_device(): lax.all_gather(token_ids, 'vocab', axis=0, tiled=True)]
  transfers between devices with their start and end apart: 3 -> 3, of which waited for: 3 -> 1; matrix products, arithmetic and copies ran while one was open for 10% -> 20% of each run, Pallas kernels for 0% -> 0%
where the time goes in v1:
time: 114 us; the launch traced here: 113 us
  waiting for transfers between devices  53.5 us (47%)
  blocking collectives  17.6 us (15%)
  matrix products  15.8 us (14%)
  between operations  15.6 us (14%)
  local copies, waits for them, and re-layouts  6.25 us (5%)
  other arithmetic  4.41 us (4%)
    all_gather x1, waiting for transfers between devices, on_device(): lax.all_gather(table, 'vocab', axis=0, tiled=True)  52.7 us
    dot_general x2, matrix products, one_block(): return jnp.dot(one_hot, grads_block, preferred_element_type=jnp.float32)  12.4 us
    all_gather x1, blocking collectives, on_device(): lax.all_gather(token_ids, 'vocab', axis=0, tiled=True)  8.88 us
    all_gather x1, blocking collectives, on_device(): lax.all_gather(token_grad, 'vocab', axis=0, tiled=True)  8.72 us
    gather x1, local copies, waits for them, and re-layouts, lookup_rows(): picked = jnp.take(piece, jnp.clip(token_ids, 0, count - 1), axis=0)  5.3 us
  transfers between devices with their start and end apart: 3, of which 1 were waited for; matrix products, arithmetic and copies ran while one was open for 20% of the time, Pallas kernels for 0%

profile of v1, /device:TPU:0, one launch (start us, length us, event | category | flops | bytes accessed | tf_op | source)
XLA Modules:
  0.0 113.3 jit_solution(647804122831928286)
XLA Ops:
  8.0 0.0 copy-start
  8.0 0.0 all-gather.5.cloned.1.call-start
  8.1 0.7 all-gather.5.cloned.1.call-update
  8.7 0.0 reduce-scatter.2.cloned.1.call-start
  8.8 0.4 copy-done
  9.2 2.1 %convolution_convert_fusion.1 = bf16[512,128]{0,1:T(8,128)(2,1)} fusion(bf16[512,1024]{1,0:T(8,128)(2,1)S(1)} %copy-done, bf16[128,1024]{1,0:T(8,128)(2,1)} %param.8), kind=kOutput, calls=%fused_computation.13 | convolution fusion | flops 134283264 | bytes 1441792 | tf_op jit(solution)/shard_map/dot_general | solution.py:40
  11.3 0.0 reduce-scatter.2.cloned.1.call-update
  11.3 0.0 all-gather.7.cloned.1.call-start
  11.4 0.7 compare_and_fusion.1
  12.1 0.7 compare_select_fusion
  12.8 52.7 %all-gather.5.cloned.1.call-done = bf16[30720,128]{1,0:T(8,128)(2,1)} async-done(((bf16[3840,128]{1,0:T(8,128)(2,1)}), bf16[30720,128]{1,0:T(8,128)(2,1)}) %all-gather.5.cloned.1.call-update) | async-done | bytes 7864336 | tf_op jit(solution)/shard_map/all_gather | solution.py:48
  65.5 5.3 %gather_fusion = bf16[512,128]{1,0:T(8,128)(2,1)S(1)} fusion(bf16[30720,128]{1,0:T(8,128)(2,1)} %all-gather.5.cloned.1.call-done, s32[1024]{0:T(1024)S(1)} %pad_clamp_fusion), kind=kCustom, calls=%fused_computation | custom fusion | bytes 264192 | tf_op jit(solution)/shard_map/jit(_take)/gather | solution.py:15
  70.8 1.3 %convolution_convert_fusion = bf16[128,1024]{1,0:T(8,128)(2,1)} fusion(bf16[512,1024]{1,0:T(8,128)(2,1)S(1)} %copy-done, bf16[512,128]{1,0:T(8,128)(2,1)S(1)} %gather_fusion, pred[512]{0:T(512)(128)(4,1)S(1)} %get-tuple-element.72, pred[512]{0:T(512)(128)(4,1)S(1)} %get-tuple-element.71), kind=kOutput, calls=%fused_computation.12 | convolution fusion | flops 134610944 | bytes 1442816 | tf_op jit(solution)/shard_map/dot_general | solution.py:50
  72.1 0.0 all-gather.7.cloned.1.call-update
  72.2 8.9 %all-gather.1 = s32[8,1,512]{2,1,0:T(1,128)S(1)} all-gather(s32[1,1,512]{2,1,0:T(1,128)} %bitcast.17), channel_id=1, replica_groups=mesh['vocab'=8,'hidden'=4] {'vocab'}, dimensions={0}, use_global_device_ids=true | all-gather | bytes 18432 | tf_op jit(solution)/shard_map/all_gather | solution.py:60
  81.1 0.0 reduce-scatter.2.cloned.1.call-done
  81.2 8.7 %all_gather.16 = bf16[4096,32]{0,1:T(8,128)(2,1)S(1)} all-gather(bf16[512,32]{0,1:T(8,128)(2,1)} %reduce-scatter.2.cloned.1.call-done), channel_id=1, replica_groups=mesh['vocab'=8,'hidden'=4] {'vocab'}, dimensions={0}, use_global_device_ids=true | all-gather | bytes 294912 | tf_op jit(solution)/shard_map/all_gather | solution.py:59
  89.9 0.5 copy.8
  90.4 12.5 %while.11 = (s32[]{:T(128)}, f32[3840,32]{0,1:T(8,128)S(1)}, s32[2,2048]{1,0:T(2,128)S(1)}, bf16[2,2048,32]{2,1,0:T(8,128)(2,1)S(1)}, s32[]{:T(128)}, /*index=5*/s32[]{:T(128)}, s32[]{:T(128)}) while((s32[]{:T(128)}, f32[3840,32]{0,1:T(8,128)S(1)}, s32[2,2048]{1,0:T(2,128)S(1)}, bf16[2,2048,32]{2,1,0:T(8,128)(2,1)S(1)}, s32[]{:T(128)}, ...), condition=%wide.region_2.3_spmd.clone, body=%wide.region_1.2_spmd.clone.sunk | while | flops 511430400 | bytes 1563747 | solution.py:35
  90.4 6.2 %fusion.27 = f32[3840,32]{0,1:T(8,128)S(1)} fusion(s32[2048]{0:T(1024)S(1)} %bitcast.16, s32[3840]{0:T(1024)S(1)} %iota_add_fusion.2, bf16[2,2048,32]{2,1,0:T(8,128)(2,1)S(1)} %get-tuple-element.121, s32[]{:T(128)} %get-tuple-element.111, f32[3840,32]{0,1:T(8,128)S(1)} %get-tuple-element.112, pred[]{:T(512)S(6)} %compare.3), kind=kOutput, calls=%fused_computation.6.clone.1 | convolution fusion | flops 511426560 | bytes 1531909 | tf_op jit(solution)/shard_map/while/body/eval_jaxpr/dot_general | solution.py:26
  96.7 6.2 %fusion.27 = f32[3840,32]{0,1:T(8,128)S(1)} fusion(s32[2048]{0:T(1024)S(1)} %bitcast.16, s32[3840]{0:T(1024)S(1)} %iota_add_fusion.2, bf16[2,2048,32]{2,1,0:T(8,128)(2,1)S(1)} %get-tuple-element.121, s32[]{:T(128)} %get-tuple-element.111, f32[3840,32]{0,1:T(8,128)S(1)} %get-tuple-element.112, pred[]{:T(512)S(6)} %compare.3), kind=kOutput, calls=%fused_computation.6.clone.1 | convolution fusion | flops 511426560 | bytes 1531909 | tf_op jit(solution)/shard_map/while/body/eval_jaxpr/dot_general | solution.py:26
  102.9 0.0 copy-start.1
  102.9 0.0 all-gather.7.cloned.1.call-done
  102.9 2.1 %reduce_sum.12 = bf16[128,1024]{1,0:T(8,128)(2,1)S(1)} reduce(bf16[8,128,1024]{2,1,0:T(8,128)(2,1)} %bitcast.14, bf16[]{:T(256)} %constant.41.clone.1), dimensions={0}, to_apply=%region_3.4 | reduce | flops 917504 | bytes 2359298 | tf_op jit(solution)/shard_map/reduce_sum | solution.py:9
  105.0 0.8 convert_element_type.24
  105.9 0.0 copy-done.1
  (8 shorter events, 0.1 us)
Async XLA Ops:
  8.0 1.2 %copy-start = (bf16[512,1024]{1,0:T(8,128)(2,1)S(1)}, bf16[512,1024]{1,0:T(8,128)(2,1)}, u32[]{:S(2)}) copy-start(bf16[512,1024]{1,0:T(8,128)(2,1)} %param.9) | copy-start | bytes 3145732
  8.0 57.5 %all-gather.5.cloned.1.call-start = ((), (), s32[]{:S(2)}) async-start(), calls=%async_computation.2 | async-start | bytes 8847360 | tf_op jit(solution)/shard_map/all_gather | solution.py:48
  8.7 72.4 %reduce-scatter.2.cloned.1.call-start = ((), (), s32[]{:S(2)}) async-start(), calls=%async_computation.1 | async-start | bytes 163840 | tf_op jit(solution)/shard_map/reduce_scatter | solution.py:43
  11.3 91.6 %all-gather.7.cloned.1.call-start = ((), (), s32[]{:S(2)}) async-start(), calls=%async_computation.3 | async-start | bytes 2359296 | tf_op jit(solution)/shard_map/all_gather | solution.py:8
  102.9 3.0 %copy-start.1 = (f32[3840,32]{0,1:T(8,128)}, f32[3840,32]{0,1:T(8,128)S(1)}, u32[]{:S(2)}) copy-start(f32[3840,32]{0,1:T(8,128)S(1)} %get-tuple-element.27) | copy-start | bytes 1474564
Sparse Core Ops, SparseCore 0:
  10.7 54.7 all-gather.4
  72.3 28.0 all-gather.6
Sparse Core Ops, SparseCore 1:
  12.0 22.1 reduce-scatter.1
